TPU v7x, 128 devices: a whole 4x4x4 slice. The times are simulated.
128 devices in a mesh: dp: 4 (over y), expert: 32 (over x, z, core).
Axes of the slice: x: 4, y: 4, z: 4, core: 2. Of those that a mesh axis runs over, the one named last changes fastest.
Arguments:
- tokens: bfloat16 [16384, 2048], P(('dp', 'expert')), may hold values from -6 to 6
- cotangent: bfloat16 [16384, 2048], P(('dp', 'expert')), may hold values from -6 to 6
- expert_ids: int32 [16384, 6], P(('dp', 'expert')), may hold values from 0 to 31, as said below
- gate_fixed: int32 [16384, 6], P(('dp', 'expert')), may hold values from 1024 to 65535
- w_gate: bfloat16 [32, 2048, 704], P('expert'), may hold values from -0.125 to 0.125
- w_up: bfloat16 [32, 2048, 704], P('expert'), may hold values from -0.125 to 0.125
- w_down: bfloat16 [32, 704, 2048], P('expert'), may hold values from -0.21875 to 0.21875
Outputs:
- mixed: bfloat16 [16384, 2048], P(('dp', 'expert'))
- token_grad: bfloat16 [16384, 2048], P(('dp', 'expert'))
- grad_gate: float32 [32, 2048, 704], P('expert', 'dp')
- grad_up: float32 [32, 2048, 704], P('expert', 'dp')
- grad_down: float32 [32, 704, 2048], P('expert', None, 'dp')
Inputs may be any that keep to these rules, and one draw needn't show every extreme that they name: `expert_ids`: each row names 6 different experts. Within the rows of one device (aligned blocks of 128 rows) no expert is named by more than 32 rows, and one expert, the same in every block, is named by exactly 32 rows.
All inputs are finite; a program needn't handle non-finite values.
Results may differ from a plain program's by a relative error of at most 0.0095.
Values may be sent and summed in bfloat16 or wider, within the bound.
A program may use at most 192 MiB of HBM per device.

v0:
```python
from functools import partial

import jax
import jax.numpy as jnp
from jax import lax
from jax.sharding import PartitionSpec as P


def contract(left, right):
    return lax.dot_general(
        left, right, (((0,), (0,)), ((), ())), preferred_element_type=jnp.float32
    )


def trans_dot(left, right):
    return lax.dot_general(
        left, right, (((1,), (1,)), ((), ())), preferred_element_type=jnp.float32
    )


def forward_rows(gate_w, up_w, down_w, rows_in):
    gate_pre = jnp.dot(rows_in, gate_w, preferred_element_type=jnp.float32)
    up_pre = jnp.dot(rows_in, up_w, preferred_element_type=jnp.float32)
    hidden = (gate_pre * jax.nn.sigmoid(gate_pre) * up_pre).astype(jnp.bfloat16)
    expert_out = jnp.dot(hidden, down_w, preferred_element_type=jnp.float32).astype(jnp.bfloat16)
    return (expert_out, gate_pre, up_pre, hidden)


def backward_rows(gate_w, up_w, down_w, dy_rows, gate_pre, up_pre):
    sigma = jax.nn.sigmoid(gate_pre)
    activ = gate_pre * sigma
    d_hidden = trans_dot(dy_rows, down_w)
    d_gate = (d_hidden * up_pre * (sigma * (1.0 + gate_pre * (1.0 - sigma)))).astype(jnp.bfloat16)
    d_up = (d_hidden * activ).astype(jnp.bfloat16)
    d_rows = (trans_dot(d_gate, gate_w) + trans_dot(d_up, up_w)).astype(jnp.bfloat16)
    return (d_rows, d_gate, d_up)


def shards(tokens, cotangent, expert_ids, gate_fixed, w_gate, w_up, w_down):
    n_expert = lax.axis_size("expert")
    tok_rows = tokens.shape[0]
    width = tokens.shape[1]
    top_k = expert_ids.shape[1]
    capacity = 4 * tok_rows * top_k // (3 * n_expert)
    slot_count = n_expert * capacity
    gate_w = w_gate[0]
    up_w = w_up[0]
    down_w = w_down[0]
    flat_ids = expert_ids.reshape(-1)
    onehot = (flat_ids[:, None] == jnp.arange(n_expert, dtype=jnp.int32)[None, :]).astype(jnp.int32)
    before = jnp.cumsum(onehot, axis=0) - onehot
    rank_in = jnp.sum(before * onehot, axis=1)
    counts = jnp.sum(onehot, axis=0)
    slot_of = flat_ids * capacity + rank_in
    owner = jnp.arange(flat_ids.shape[0], dtype=jnp.int32) // top_k
    slot_token = jnp.zeros((slot_count,), jnp.int32).at[slot_of].set(owner)
    gate_values = gate_fixed.reshape(-1).astype(jnp.float32) / 65536.0
    slot_gate = jnp.zeros((slot_count,), jnp.float32).at[slot_of].set(gate_values)
    outgoing = jnp.where(
        (slot_gate > 0.0)[:, None], tokens[slot_token], jnp.zeros((), tokens.dtype)
    )
    received, arrived = (
        lax.all_to_all(outgoing, "expert", split_axis=0, concat_axis=0, tiled=True),
        lax.all_to_all(counts, "expert", split_axis=0, concat_axis=0, tiled=True),
    )

    def run_rows(row_fn, inputs):
        return row_fn(*inputs)

    def fold_rows(left, right):
        return contract(left, right)

    expert_out, gate_pre, up_pre, hidden = run_rows(
        partial(forward_rows, gate_w, up_w, down_w), (received,)
    )
    returned = lax.all_to_all(expert_out, "expert", split_axis=0, concat_axis=0, tiled=True)
    mixed_rows = returned[slot_of].astype(jnp.float32).reshape(tok_rows, top_k, width)
    mixed = jnp.sum(mixed_rows * gate_values.reshape(tok_rows, top_k)[:, :, None], axis=1).astype(
        jnp.bfloat16
    )
    dy_out = (cotangent[slot_token].astype(jnp.float32) * slot_gate[:, None]).astype(jnp.bfloat16)
    dy_in = lax.all_to_all(dy_out, "expert", split_axis=0, concat_axis=0, tiled=True)
    d_rows, d_gate, d_up = run_rows(
        partial(backward_rows, gate_w, up_w, down_w), (dy_in, gate_pre, up_pre)
    )
    back_rows = lax.all_to_all(d_rows, "expert", split_axis=0, concat_axis=0, tiled=True)
    token_grad = jnp.sum(
        back_rows[slot_of].astype(jnp.float32).reshape(tok_rows, top_k, width), axis=1
    ).astype(jnp.bfloat16)
    grad_gate, grad_up, grad_down = (
        lax.psum_scatter(
            fold_rows(received, d_gate).astype(jnp.bfloat16), "dp", scatter_dimension=0, tiled=True
        ).astype(jnp.float32),
        lax.psum_scatter(
            fold_rows(received, d_up).astype(jnp.bfloat16), "dp", scatter_dimension=0, tiled=True
        ).astype(jnp.float32),
        lax.psum_scatter(
            fold_rows(hidden, dy_in).astype(jnp.bfloat16), "dp", scatter_dimension=1, tiled=True
        ).astype(jnp.float32),
    )
    return (mixed, token_grad, grad_gate[None], grad_up[None], grad_down[None])


def solution(mesh):
    in_specs = (
        P(("dp", "expert"), None),
        P(("dp", "expert"), None),
        P(("dp", "expert"), None),
        P(("dp", "expert"), None),
        P("expert", None, None),
        P("expert", None, None),
        P("expert", None, None),
    )
    out_specs = (
        P(("dp", "expert"), None),
        P(("dp", "expert"), None),
        P("expert", "dp", None),
        P("expert", "dp", None),
        P("expert", None, "dp"),
    )
    return jax.shard_map(shards, mesh=mesh, in_specs=in_specs, out_specs=out_specs, check_vma=False)
```

profile of v0, /device:TPU:1, one launch (start us, length us, event | category | flops | bytes accessed | tf_op | source)
XLA Modules:
  0.0 346.8 jit_solution(405778989388814010)
XLA Ops:
  11.7 3.3 reduce-window.6
  15.4 3.5 %scatter_custom_fusion.1 = s32[1024]{0:T(1024)S(1)} fusion(s32[768]{0:T(1024)S(1)} %fusion.20, s32[768]{0:T(1024)} %add_select_fusion, s32[]{:T(128)} %constant.9.clone.1), kind=kCustom, calls=%fused_computation.55 | custom fusion | bytes 4608 | tf_op jit(solution)/shard_map/scatter | solution.py:56
  18.9 3.4 scatter_custom_fusion
  22.4 6.0 %gather_fusion = bf16[1024,2048]{1,0:T(8,128)(2,1)} fusion(bf16[128,2048]{1,0:T(8,128)(2,1)S(1)} %copy-done.2, s32[1024]{0:T(1024)S(1)} %fusion.18), kind=kCustom, calls=%fused_computation | custom fusion | bytes 8392704 | tf_op jit(solution)/shard_map/gather | solution.py:60
  28.4 4.5 %broadcast_select_fusion = bf16[32,32,2048]{2,1,0:T(8,128)(2,1)} fusion(bf16[32,32,2048]{2,1,0:T(8,128)(2,1)} %bitcast.70, pred[32,32]{1,0:T(8,128)(4,1)S(1)} %broadcast_in_dim.43), kind=kLoop, calls=%fused_computation.10 | loop fusion | flops 2097152 | bytes 8389632 | tf_op jit(solution)/shard_map/jit(_where)/select_n | solution.py:59
  32.9 9.6 %all-to-all-start = ((bf16[32,32,2048]{2,1,0:T(8,128)(2,1)}), bf16[32,32,2048]{2,1,0:T(8,128)(2,1)}, u32[]{:S(2)}, u32[]{:S(2)}) async-start(bf16[32,32,2048]{2,1,0:T(8,128)(2,1)} %broadcast_select_fusion), calls=%async_computation | async-start | bytes 8388608 | tf_op jit(solution)/shard_map/all_to_all | solution.py:63
  42.6 6.0 %gather_fusion.2 = bf16[1024,2048]{1,0:T(8,128)(2,1)} fusion(bf16[128,2048]{1,0:T(8,128)(2,1)S(1)} %copy-done.3, s32[1024]{0:T(1024)S(1)} %fusion.18), kind=kCustom, calls=%fused_computation.2 | custom fusion | bytes 8392704 | tf_op jit(solution)/shard_map/gather | solution.py:81
  48.6 4.9 %fusion = bf16[32,32,2048]{2,1,0:T(8,128)(2,1)} fusion(bf16[32,32,2048]{2,1,0:T(8,128)(2,1)} %bitcast.69, f32[32,32]{1,0:T(8,128)S(1)} %mul.68), kind=kLoop, calls=%fused_computation.7 | loop fusion | flops 6291456 | bytes 8392704 | tf_op jit(solution)/shard_map/convert_element_type | solution.py:81
  53.5 41.1 %all-to-all-done = bf16[32,32,2048]{2,1,0:T(8,128)(2,1)} async-done(((bf16[32,32,2048]{2,1,0:T(8,128)(2,1)}), bf16[32,32,2048]{2,1,0:T(8,128)(2,1)}, u32[]{:S(2)}, u32[]{:S(2)}) %all-to-all-start) | async-done | bytes 4194336 | tf_op jit(solution)/shard_map/all_to_all | solution.py:63
  94.7 7.1 %all-to-all-start.2 = ((bf16[32,32,2048]{2,1,0:T(8,128)(2,1)}), bf16[32,32,2048]{2,1,0:T(8,128)(2,1)}, u32[]{:S(2)}, u32[]{:S(2)}) async-start(bf16[32,32,2048]{2,1,0:T(8,128)(2,1)} %fusion), calls=%async_computation.2 | async-start | bytes 8388608 | tf_op jit(solution)/shard_map/all_to_all | solution.py:82
  102.1 8.0 %fusion.5 = f32[1024,704]{0,1:T(8,128)} fusion(bf16[1024,2048]{1,0:T(8,128)(2,1)} %bitcast.2, bf16[1,2048,704]{1,2,0:T(8,128)(2,1)} %param.12), kind=kOutput, calls=%fused_computation.19 | convolution fusion | flops 2952790016 | bytes 9961472 | tf_op jit(solution)/shard_map/dot_general | solution.py:23
  110.1 6.9 %fusion.9 = f32[1024,704]{0,1:T(8,128)} fusion(bf16[1024,2048]{1,0:T(8,128)(2,1)} %bitcast.2, bf16[1,2048,704]{1,2,0:T(8,128)(2,1)S(1)} %copy-done.6), kind=kOutput, calls=%fused_computation.23 | convolution fusion | flops 2952790016 | bytes 9961472 | tf_op jit(solution)/shard_map/dot_general | solution.py:22
  117.0 36.9 %all-to-all-done.2 = bf16[32,32,2048]{2,1,0:T(8,128)(2,1)} async-done(((bf16[32,32,2048]{2,1,0:T(8,128)(2,1)}), bf16[32,32,2048]{2,1,0:T(8,128)(2,1)}, u32[]{:S(2)}, u32[]{:S(2)}) %all-to-all-start.2) | async-done | bytes 4194336 | tf_op jit(solution)/shard_map/all_to_all | solution.py:82
  153.9 8.5 %multiply_convert_fusion = (bf16[1024,704]{0,1:T(8,128)(2,1)}, bf16[1024,704]{0,1:T(8,128)(2,1)}, bf16[1024,704]{0,1:T(8,128)(2,1)S(1)}) fusion(f32[1024,704]{0,1:T(8,128)} %fusion.9, f32[1024,704]{0,1:T(8,128)} %fusion.5, bf16[1024,2048]{1,0:T(8,128)(2,1)} %bitcast.9, bf16[1,704,2048]{2,1,0:T(8,128)(2,1)S(1)} %copy-done), kind=kOutput, calls=%fused_computation.25 | convolution fusion | flops 2963603456 | bytes 17170432 | tf_op jit(solution)/shard_map/dot_general | solution.py:16
  163.5 6.7 %convolution_convert_fusion.3 = bf16[704,2048]{1,0:T(8,128)(2,1)} fusion(bf16[1024,704]{0,1:T(8,128)(2,1)S(1)} %get-tuple-element.7, bf16[1024,2048]{1,0:T(8,128)(2,1)} %bitcast.9), kind=kOutput, calls=%fused_computation.14 | convolution fusion | flops 2954231808 | bytes 8519680 | tf_op jit(solution)/shard_map/dot_general | solution.py:10
  170.8 7.4 %convolution_convert_fusion.1 = bf16[2048,704]{0,1:T(8,128)(2,1)} fusion(bf16[1024,704]{0,1:T(8,128)(2,1)} %get-tuple-element.5, bf16[1024,2048]{1,0:T(8,128)(2,1)} %bitcast.2), kind=kOutput, calls=%fused_computation.12 | convolution fusion | flops 2954231808 | bytes 8519680 | tf_op jit(solution)/shard_map/dot_general | solution.py:10
  178.2 6.4 %convolution_convert_fusion = bf16[1024,2048]{1,0:T(8,128)(2,1)} fusion(bf16[1024,704]{0,1:T(8,128)(2,1)} %copy-done.11, bf16[1,704,2048]{2,1,0:T(8,128)(2,1)S(1)} %copy-done), kind=kOutput, calls=%fused_computation.11 | convolution fusion | flops 2954887168 | bytes 8519680 | tf_op jit(solution)/shard_map/dot_general | solution.py:25
  184.6 7.2 %all-to-all-start.1 = ((bf16[32,32,2048]{2,1,0:T(8,128)(2,1)}), bf16[32,32,2048]{2,1,0:T(8,128)(2,1)}, u32[]{:S(2)}, u32[]{:S(2)}) async-start(bf16[32,32,2048]{2,1,0:T(8,128)(2,1)} %bitcast.71), calls=%async_computation.1 | async-start | bytes 8388608 | tf_op jit(solution)/shard_map/all_to_all | solution.py:76
  191.9 6.7 %convolution_convert_fusion.2 = bf16[2048,704]{0,1:T(8,128)(2,1)} fusion(bf16[1024,704]{0,1:T(8,128)(2,1)S(1)} %copy-done.9, bf16[1024,2048]{1,0:T(8,128)(2,1)} %bitcast.2), kind=kOutput, calls=%fused_computation.13 | convolution fusion | flops 2954231808 | bytes 8519680 | tf_op jit(solution)/shard_map/dot_general | solution.py:10
  200.4 5.1 %fusion.7 = f32[1024,2048]{1,0:T(8,128)S(1)} fusion(bf16[1024,704]{0,1:T(8,128)(2,1)} %get-tuple-element.6, bf16[1,2048,704]{1,2,0:T(8,128)(2,1)S(1)} %copy-done.7), kind=kOutput, calls=%fused_computation.21 | convolution fusion | flops 2952790016 | bytes 12713984 | tf_op jit(solution)/shard_map/dot_general | solution.py:16
  205.5 5.4 %add_convert_fusion = bf16[1024,2048]{1,0:T(8,128)(2,1)} fusion(f32[1024,2048]{1,0:T(8,128)S(1)} %fusion.7, bf16[1024,704]{0,1:T(8,128)(2,1)S(1)} %copy-done.10, bf16[1,2048,704]{1,2,0:T(8,128)(2,1)S(1)} %copy-done.8), kind=kOutput, calls=%fused_computation.8 | convolution fusion | flops 2956984320 | bytes 16908288 | tf_op jit(solution)/shard_map/dot_general | solution.py:16
  210.8 33.1 %all-to-all-done.1 = bf16[32,32,2048]{2,1,0:T(8,128)(2,1)} async-done(((bf16[32,32,2048]{2,1,0:T(8,128)(2,1)}), bf16[32,32,2048]{2,1,0:T(8,128)(2,1)}, u32[]{:S(2)}, u32[]{:S(2)}) %all-to-all-start.1) | async-done | bytes 4194336 | tf_op jit(solution)/shard_map/all_to_all | solution.py:76
  243.9 7.4 %all-to-all-start.3 = ((bf16[32,32,2048]{2,1,0:T(8,128)(2,1)}), bf16[32,32,2048]{2,1,0:T(8,128)(2,1)}, u32[]{:S(2)}, u32[]{:S(2)}) async-start(bf16[32,32,2048]{2,1,0:T(8,128)(2,1)} %bitcast.72), calls=%async_computation.3 | async-start | bytes 8388608 | tf_op jit(solution)/shard_map/all_to_all | solution.py:86
  251.4 9.8 %gather_fusion.1 = bf16[768,2048]{1,0:T(8,128)(2,1)} fusion(bf16[1024,2048]{1,0:T(8,128)(2,1)} %bitcast.7, s32[1024]{0:T(1024)S(1)} %pad_clamp_fusion), kind=kCustom, calls=%fused_computation.1 | custom fusion | bytes 6294528 | tf_op jit(solution)/shard_map/gather | solution.py:77
  261.2 6.6 %reshape.95 = f32[128,6,2048]{2,1,0:T(8,128)} reshape(bf16[768,2048]{1,0:T(8,128)(2,1)} %gather_fusion.1) | data formatting | bytes 9437184 | tf_op jit(solution)/shard_map/convert_element_type | solution.py:77
  267.8 35.5 %all-to-all-done.3 = bf16[32,32,2048]{2,1,0:T(8,128)(2,1)} async-done(((bf16[32,32,2048]{2,1,0:T(8,128)(2,1)}), bf16[32,32,2048]{2,1,0:T(8,128)(2,1)}, u32[]{:S(2)}, u32[]{:S(2)}) %all-to-all-start.3) | async-done | bytes 4194336 | tf_op jit(solution)/shard_map/all_to_all | solution.py:86
  303.3 9.8 %gather_fusion.3 = bf16[768,2048]{1,0:T(8,128)(2,1)} fusion(bf16[1024,2048]{1,0:T(8,128)(2,1)} %bitcast.11, s32[1024]{0:T(1024)S(1)} %pad_clamp_fusion), kind=kCustom, calls=%fused_computation.3 | custom fusion | bytes 6294528 | tf_op jit(solution)/shard_map/gather | solution.py:88
  313.1 6.4 %gather.21 = bf16[128,6,2048]{2,1,0:T(8,128)(2,1)} reshape(bf16[768,2048]{1,0:T(8,128)(2,1)} %gather_fusion.3) | data formatting | bytes 6291456 | tf_op jit(solution)/shard_map/gather | solution.py:88
  319.6 5.7 %reduce_sum.35 = bf16[128,2048]{1,0:T(8,128)(2,1)} reduce(bf16[128,6,2048]{2,1,0:T(8,128)(2,1)} %gather.21, bf16[]{:T(256)} %constant.33.clone.1), dimensions={1}, to_apply=%region_6.7 | reduce | flops 1310720 | bytes 3670018 | tf_op jit(solution)/shard_map/reduce_sum | solution.py:87
  325.3 7.5 %multiply_reduce_fusion = bf16[128,2048]{1,0:T(8,128)(2,1)} fusion(f32[128,6,2048]{2,1,0:T(8,128)} %reshape.95, f32[128,6]{1,0:T(8,128)S(1)} %copy-done.5), kind=kLoop, calls=%fused_computation.9 | loop fusion | flops 2883584 | bytes 6818816 | tf_op jit(solution)/shard_map/reduce_sum | solution.py:78
  332.8 2.4 bitcast_convert_fusion
  337.7 2.4 bitcast_convert_fusion.2
  (54 shorter events, 11.3 us)
Async XLA Ops:
  7.2 146.7 %copy-start = (bf16[1,704,2048]{2,1,0:T(8,128)(2,1)S(1)}, bf16[1,704,2048]{2,1,0:T(8,128)(2,1)}, u32[]{:S(2)}) copy-start(bf16[1,704,2048]{2,1,0:T(8,128)(2,1)} %param.13) | copy-start | bytes 8650756
  7.2 15.2 %copy-start.2 = (bf16[128,2048]{1,0:T(8,128)(2,1)S(1)}, bf16[128,2048]{1,0:T(8,128)(2,1)}, u32[]{:S(2)}) copy-start(bf16[128,2048]{1,0:T(8,128)(2,1)} %param.7) | copy-start | bytes 1572868
  10.4 0.6 copy-start.4
  32.9 9.7 %copy-start.3 = (bf16[128,2048]{1,0:T(8,128)(2,1)S(1)}, bf16[128,2048]{1,0:T(8,128)(2,1)}, u32[]{:S(2)}) copy-start(bf16[128,2048]{1,0:T(8,128)(2,1)} %param.8) | copy-start | bytes 1572868
  32.9 61.7 %all-to-all-start = ((bf16[32,32,2048]{2,1,0:T(8,128)(2,1)}), bf16[32,32,2048]{2,1,0:T(8,128)(2,1)}, u32[]{:S(2)}, u32[]{:S(2)}) async-start(bf16[32,32,2048]{2,1,0:T(8,128)(2,1)} %broadcast_select_fusion), calls=%async_computation | async-start | bytes 8388608 | tf_op jit(solution)/shard_map/all_to_all | solution.py:63
  94.7 59.2 %all-to-all-start.2 = ((bf16[32,32,2048]{2,1,0:T(8,128)(2,1)}), bf16[32,32,2048]{2,1,0:T(8,128)(2,1)}, u32[]{:S(2)}, u32[]{:S(2)}) async-start(bf16[32,32,2048]{2,1,0:T(8,128)(2,1)} %fusion), calls=%async_computation.2 | async-start | bytes 8388608 | tf_op jit(solution)/shard_map/all_to_all | solution.py:82
  101.8 231.1 %reduce-scatter.8.cloned.1.call-start = ((), (), s32[]{:S(2)}) async-start(), calls=%async_computation.9 | async-start | bytes 3604480 | tf_op jit(solution)/shard_map/reduce_scatter | solution.py:97
  102.1 8.0 %copy-start.6 = (bf16[1,2048,704]{1,2,0:T(8,128)(2,1)S(1)}, bf16[1,2048,704]{1,2,0:T(8,128)(2,1)}, u32[]{:S(2)}) copy-start(bf16[1,2048,704]{1,2,0:T(8,128)(2,1)} %param.11) | copy-start | bytes 8650756
  162.4 1.1 copy-start.11
  170.2 165.1 %reduce-scatter.6.cloned.1.call-start = ((), (), s32[]{:S(2)}) async-start(), calls=%async_computation.8 | async-start | bytes 3604480 | tf_op jit(solution)/shard_map/reduce_scatter | solution.py:94
  184.6 7.3 %copy-start.9 = (bf16[1024,704]{0,1:T(8,128)(2,1)S(1)}, bf16[1024,704]{0,1:T(8,128)(2,1)}, u32[]{:S(2)}) copy-start(bf16[1024,704]{0,1:T(8,128)(2,1)} %get-tuple-element.6) | copy-start | bytes 4325380
  184.6 59.3 %all-to-all-start.1 = ((bf16[32,32,2048]{2,1,0:T(8,128)(2,1)}), bf16[32,32,2048]{2,1,0:T(8,128)(2,1)}, u32[]{:S(2)}, u32[]{:S(2)}) async-start(bf16[32,32,2048]{2,1,0:T(8,128)(2,1)} %bitcast.71), calls=%async_computation.1 | async-start | bytes 8388608 | tf_op jit(solution)/shard_map/all_to_all | solution.py:76
  191.8 145.8 %reduce-scatter.4.cloned.1.call-start = ((), (), s32[]{:S(2)}) async-start(), calls=%async_computation.7 | async-start | bytes 3604480 | tf_op jit(solution)/shard_map/reduce_scatter | solution.py:91
  198.6 1.8 copy-start.7
  200.4 5.1 %copy-start.8 = (bf16[1,2048,704]{1,2,0:T(8,128)(2,1)S(1)}, bf16[1,2048,704]{1,2,0:T(8,128)(2,1)}, u32[]{:S(2)}) copy-start(bf16[1,2048,704]{1,2,0:T(8,128)(2,1)} %param.12) | copy-start | bytes 8650756
  200.4 5.1 %copy-start.10 = (bf16[1024,704]{0,1:T(8,128)(2,1)S(1)}, bf16[1024,704]{0,1:T(8,128)(2,1)}, u32[]{:S(2)}) copy-start(bf16[1024,704]{0,1:T(8,128)(2,1)} %get-tuple-element.5) | copy-start | bytes 4325380
  243.9 59.4 %all-to-all-start.3 = ((bf16[32,32,2048]{2,1,0:T(8,128)(2,1)}), bf16[32,32,2048]{2,1,0:T(8,128)(2,1)}, u32[]{:S(2)}, u32[]{:S(2)}) async-start(bf16[32,32,2048]{2,1,0:T(8,128)(2,1)} %bitcast.72), calls=%async_computation.3 | async-start | bytes 8388608 | tf_op jit(solution)/shard_map/all_to_all | solution.py:86
  319.6 5.7 %copy-start.5 = (f32[128,6]{1,0:T(8,128)S(1)}, f32[128,6]{1,0:T(8,128)}, u32[]{:S(2)}) copy-start(f32[128,6]{1,0:T(8,128)} %copy-done.4) | copy-start | bytes 9220
  325.3 14.8 %copy-start.1 = (bf16[1,704,2048]{2,1,0:T(8,128)(2,1)S(1)}, bf16[1,704,2048]{2,1,0:T(8,128)(2,1)}, u32[]{:S(2)}) copy-start(bf16[1,704,2048]{2,1,0:T(8,128)(2,1)} %param.13) | copy-start | bytes 8650756
Sparse Core Ops, SparseCore 0:
  170.3 36.8 reduce-scatter.7
  209.6 35.8 reduce-scatter.5
  247.9 35.8 reduce-scatter.3
where the time goes:
time: 353 us; the launch traced here: 347 us
  waiting for transfers between devices  147 us (42%)
  matrix products  61 us (17%)
  local copies, waits for them, and re-layouts  56.7 us (16%)
  other arithmetic  36 us (10%)
  starting transfers between devices  32.3 us (9%)
  between operations  14.2 us (4%)
    all_to_all x1, waiting for transfers between devices, shards(): lax.all_to_all(outgoing, 'expert', split_axis=0, concat_axis=0, tiled=True)  41.1 us
    all_to_all x1, waiting for transfers between devices, shards(): lax.all_to_all(dy_out, 'expert', split_axis=0, concat_axis=0, tiled=True)  36.9 us
    all_to_all x1, waiting for transfers between devices, shards(): lax.all_to_all(d_rows, 'expert', split_axis=0, concat_axis=0, tiled=True)  35.5 us
    all_to_all x1, waiting for transfers between devices, shards(): lax.all_to_all(expert_out, 'expert', split_axis=0, concat_axis=0, tiled=T...  33.1 us
    dot_general x3, matrix products, contract(): lax.dot_general(left, right, (((0,), (0,)), ((), ())), preferred_element_...  20.8 us
    dot_general x3, matrix products, trans_dot(): lax.dot_general(left, right, (((1,), (1,)), ((), ())), preferred_element_...  18.9 us
    gather x2, local copies, waits for them, and re-layouts, shards(): back_rows[slot_of].astype(jnp.float32).reshape(tok_rows, top_k, width)  16.3 us
    gather x1, local copies, waits for them, and re-layouts, shards(): returned[slot_of].astype(jnp.float32).reshape(tok_rows, top_k, width)  9.83 us
  transfers between devices with their start and end apart: 7, of which 4 were waited for; matrix products, arithmetic and copies ran while one was open for 31% of the time, Pallas kernels for 0%

commit v1 on v0

v1 whole, which is shorter than its diff:
```python
import functools

import jax
import jax.numpy as jnp
from jax import lax
from jax.experimental import pallas as pl
from jax.experimental.pallas import tpu as pltpu
from jax.sharding import PartitionSpec as P

MESH = pl.DeviceIdType.MESH
CAP = 32
BF = jnp.bfloat16
F32 = jnp.float32


def dot_nn(a, b):
    return lax.dot_general(a, b, (((1,), (0,)), ((), ())), preferred_element_type=F32)


def dot_nt(a, b):
    return lax.dot_general(a, b, (((1,), (1,)), ((), ())), preferred_element_type=F32)


def dot_tn(a, b):
    return lax.dot_general(a, b, (((0,), (0,)), ((), ())), preferred_element_type=F32)


def layer(n, top, tab, tok, cot, wg, wu, wd, mixed, tgrad, gg, gu, gd, rs2,
          w, s1, tb, pb, pg, snd, rows, rel, prec, ownp, h_t, fa, fb, gs, rs1,
          in_sem, s1_s, s1_r, tb_s, tb_r, s2_s, s2_r, rt_s, rt_r, r1_s, r1_r,
          rs_s, rs_r, loc):
    tokens, width = tok.shape
    half = width // 2
    ff = w.shape[1]
    fh = ff // 2
    quart = width // 4
    blk = 2 * n * CAP
    slots = n * blk
    y = lax.axis_index("dp")
    e = lax.axis_index("expert")
    x = e // (2 * n)
    z = lax.rem(e // 2, n)
    c = lax.rem(e, 2)

    def dev(xx, zz, cc):
        return (y, xx * (2 * n) + zz * 2 + cc)

    def up(v, d):
        return lax.rem(v + d, n)

    def down(v, d):
        return lax.rem(v + n - d, n)

    def ring(hf, d):
        return dev(up(x, d), z, c) if hf == 0 else dev(x, up(z, d), c)

    def ring_back(hf, d):
        return dev(down(x, d), z, c) if hf == 0 else dev(x, down(z, d), c)

    y_up = lax.rem(y + 1, 4)
    y_dn = lax.rem(y + 3, 4)
    offsets = [(d, k) for d in range(n) for k in range(2) if (d, k) != (0, 0)]

    pltpu.make_async_copy(tab, tb.at[0, 0], in_sem.at[0]).start()
    pltpu.make_async_copy(tab, tb.at[1, 0], in_sem.at[1]).start()
    ins = []
    for t, src in enumerate((tok, cot)):
        for hf in range(2):
            cp = pltpu.make_async_copy(
                src.at[:, pl.ds(hf * half, half)], s1.at[t, hf, 0], in_sem.at[2 + 2 * t + hf])
            cp.start()
            ins.append(cp)
    wcp = []
    for i, src in enumerate((wg, wu, wd)):
        cp = pltpu.make_async_copy(src, w.at[i], in_sem.at[6 + i])
        cp.start()
        wcp.append(cp)

    bar = pltpu.get_barrier_semaphore()
    partners = []
    for d, k in offsets:
        partners.append(dev(x, up(z, d), lax.rem(c + k, 2)))
        if d > 0:
            partners.append(dev(up(x, d), z, lax.rem(c + k, 2)))
    partners.append((y_up, e))
    partners.append((y_dn, e))
    for p in partners:
        pl.semaphore_signal(bar, inc=1, device_id=p, device_id_type=MESH)
    pl.semaphore_wait(bar, len(partners))

    def remote(src, dst, s, r, d):
        return pltpu.make_async_remote_copy(
            src_ref=src, dst_ref=dst, send_sem=s, recv_sem=r, device_id=d, device_id_type=MESH)

    def tab_copy(hf, d):
        return remote(tb.at[hf, 0], tb.at[hf, d], tb_s.at[hf, d - 1], tb_r.at[hf, d - 1], ring(hf, d))

    def s1_copy(t, hf, d):
        return remote(s1.at[t, hf, 0], s1.at[t, hf, d], s1_s.at[t, hf, d - 1],
                      s1_r.at[t, hf, d - 1], ring(hf, d))

    pltpu.make_async_copy(tab, tb.at[0, 0], in_sem.at[0]).wait()
    pltpu.make_async_copy(tab, tb.at[1, 0], in_sem.at[1]).wait()
    for hf in range(2):
        for d in range(1, n):
            tab_copy(hf, d).start()
    for hf in range(2):
        ins[hf].wait()
        for d in range(1, n):
            s1_copy(0, hf, d).start()

    upper = (lax.broadcasted_iota(jnp.int32, (tokens, tokens), 0)
             < lax.broadcasted_iota(jnp.int32, (tokens, tokens), 1))
    upper = jnp.where(upper, 1.0, 0.0).astype(BF)
    row16 = lax.broadcasted_iota(jnp.int32, (16, tokens), 0)
    slot_no = lax.broadcasted_iota(jnp.int32, (CAP, tokens), 0).astype(F32)

    def make_p(hf, d):
        if hf == 0:
            names = x * (2 * n) + row16
        else:
            names = lax.shift_right_logical(row16, 1) * (2 * n) + z * 2 + lax.bitwise_and(row16, 1)
        table = tb[hf, d]
        hit = jnp.zeros((16, tokens), F32)
        gate = jnp.zeros((16, tokens), jnp.int32)
        for k in range(top):
            same = table[k:k + 1, :] == names
            hit = jnp.where(same, 1.0, hit)
            gate = jnp.where(same, table[8 + k:9 + k, :], gate)
        rank = dot_nn(hit.astype(BF), upper)
        rank = jnp.where(hit > 0.0, rank, -1.0)
        high = (lax.shift_right_logical(gate, 8) * 256).astype(F32)
        low = lax.bitwise_and(gate, 255).astype(F32)
        for i in range(2 * n):
            one = slot_no == rank[i:i + 1, :]
            at = pl.ds(i * CAP, CAP)
            pb[hf, d, at, :] = jnp.where(one, 1.0, 0.0).astype(BF)
            pg[hf, d, at, pl.ds(0, tokens)] = jnp.where(one, high[i:i + 1, :], 0.0).astype(BF)
            pg[hf, d, at, pl.ds(tokens, tokens)] = jnp.where(one, low[i:i + 1, :], 0.0).astype(BF)

    def relay_out(t, hf, d):
        at = down(x if hf == 0 else z, d)
        src = s1[t, hf, d]
        if t == 0:
            picked = dot_nn(pb[hf, d], src)
        else:
            picked = dot_nn(pg[hf, d], jnp.concatenate([src, src], axis=0)) * (1.0 / 65536.0)
        snd[t, hf, :, :, at] = picked.astype(BF).reshape(n, 2, CAP, half)

    for hf in range(2):
        make_p(hf, 0)
        relay_out(0, hf, 0)

    @pl.loop(1, n)
    def _(d):
        for hf in range(2):
            tab_copy(hf, d).wait()
            make_p(hf, d)

    @pl.loop(1, n)
    def _(d):
        for hf in range(2):
            s1_copy(0, hf, d).wait()

    for hf in range(2):
        ins[2 + hf].wait()
        for d in range(1, n):
            s1_copy(1, hf, d).start()

    @pl.loop(1, n)
    def _(d):
        for hf in range(2):
            relay_out(0, hf, d)

    def s2_copy(t, hf, d, k):
        j = 2 * d + k - 1
        cd = lax.rem(c + k, 2)
        if hf == 0:
            zd = up(z, d)
            return remote(snd.at[t, 0, zd, cd], rows.at[t, 0, z, c], s2_s.at[t, 0, j],
                          s2_r.at[t, 0, j], dev(x, zd, cd))
        xd = up(x, d)
        return remote(snd.at[t, 1, xd, cd], rows.at[t, 1, :, c, x], s2_s.at[t, 1, j],
                      s2_r.at[t, 1, j], dev(xd, z, cd))

    def s2_wait(t, hf, d, k):
        j = 2 * d + k - 1
        cf = lax.rem(c + k, 2)
        if hf == 0:
            land = rows.at[t, 0, down(z, d), cf]
        else:
            land = rows.at[t, 1, :, cf, down(x, d)]
        remote(land, land, s2_s.at[t, hf, j], s2_r.at[t, hf, j], dev(x, up(z, 1), c)).wait_recv()

    def s2_self(t, hf):
        if hf == 0:
            return pltpu.make_async_copy(snd.at[t, 0, z, c], rows.at[t, 0, z, c], loc.at[t, 0])
        return pltpu.make_async_copy(snd.at[t, 1, x, c], rows.at[t, 1, :, c, x], loc.at[t, 1])

    def s2_start(t):
        for d, k in offsets:
            for hf in range(2):
                s2_copy(t, hf, d, k).start()
        for hf in range(2):
            s2_self(t, hf).start()

    def s2_finish(t):
        for d, k in offsets:
            for hf in range(2):
                s2_wait(t, hf, d, k)
        for hf in range(2):
            s2_self(t, hf).wait()

    def s2_drain(t):
        for d, k in offsets:
            for hf in range(2):
                s2_copy(t, hf, d, k).wait_send()

    s2_start(0)
    for hf in range(2):
        relay_out(1, hf, 0)

    @pl.loop(1, n)
    def _(d):
        for hf in range(2):
            s1_copy(1, hf, d).wait()
            relay_out(1, hf, d)

    for cp in wcp:
        cp.wait()
    s2_finish(0)
    s2_start(1)
    s2_drain(0)

    @pl.loop(0, n)
    def _(b):
        cols = pl.ds(pl.multiple_of(b * blk, blk), blk)

        @pl.loop(0, 2)
        def _(f):
            part = pl.ds(pl.multiple_of(f * fh, fh), fh)
            xa = rows[0, 0, b].reshape(blk, half)
            xb = rows[0, 1, b].reshape(blk, half)
            gate = dot_nt(w[0, part, :half], xa) + dot_nt(w[0, part, half:], xb)
            upv = dot_nt(w[1, part, :half], xa) + dot_nt(w[1, part, half:], xb)
            s = jax.nn.sigmoid(gate)
            act = gate * s
            h_t[part, cols] = (act * upv).astype(BF)
            fa[part, cols] = (upv * (s * (1.0 + gate * (1.0 - s)))).astype(BF)
            fb[part, cols] = act.astype(BF)

        hid = h_t[:, cols]
        for hf in range(2):
            out = dot_tn(hid, w[2, :, hf * half:(hf + 1) * half])
            snd[0, hf, b] = out.astype(BF).reshape(2, n, CAP, half)

    def rt_copy(t, hf, d, k):
        j = 2 * d + k - 1
        cd = lax.rem(c + k, 2)
        if hf == 0:
            zd = up(z, d)
            return remote(snd.at[t, 0, zd, cd], rel.at[t, 0, z * 2 + c], rt_s.at[t, 0, j],
                          rt_r.at[t, 0, j], dev(x, zd, cd))
        xd = up(x, d)
        return remote(snd.at[t, 1, :, cd, xd], rel.at[t, 1, x * 2 + c], rt_s.at[t, 1, j],
                      rt_r.at[t, 1, j], dev(xd, z, cd))

    def rt_wait(t, hf, d, k):
        j = 2 * d + k - 1
        cf = lax.rem(c + k, 2)
        land = rel.at[t, hf, down(z if hf == 0 else x, d) * 2 + cf]
        remote(land, land, rt_s.at[t, hf, j], rt_r.at[t, hf, j], dev(x, up(z, 1), c)).wait_recv()

    def rt_self(t, hf):
        if hf == 0:
            return pltpu.make_async_copy(snd.at[t, 0, z, c], rel.at[t, 0, z * 2 + c], loc.at[2 + t, 0])
        return pltpu.make_async_copy(snd.at[t, 1, :, c, x], rel.at[t, 1, x * 2 + c], loc.at[2 + t, 1])

    def rt_start(t):
        for d, k in offsets:
            for hf in range(2):
                rt_copy(t, hf, d, k).start()
        for hf in range(2):
            rt_self(t, hf).start()

    def rt_finish(t):
        for d, k in offsets:
            for hf in range(2):
                rt_wait(t, hf, d, k)
        for hf in range(2):
            rt_self(t, hf).wait()

    def rt_drain(t):
        for d, k in offsets:
            for hf in range(2):
                rt_copy(t, hf, d, k).wait_send()

    rt_start(0)
    s2_finish(1)

    def quarter(i, left, t, q, f):
        part = pl.ds(pl.multiple_of(f * fh, fh), fh)
        cols = pl.ds(pl.multiple_of(lax.rem(q, 2) * quart, quart), quart)
        right = rows[t, q // 2, :, :, :, :, cols].reshape(slots, quart)
        return part, dot_nn(left[part, :], right)

    def rs_first(i, way):
        part = pl.ds(way * fh, fh)
        return remote(gs.at[i, 0, part], rs1.at[i, way], rs_s.at[i, way], rs_r.at[i, way],
                      (y_up if way == 0 else y_dn, e))

    def rs_second(i, way, f):
        part = pl.ds(f * fh, fh)
        j = 2 + 2 * way + f
        return remote(gs.at[i, 1 + way, part], rs2.at[i, way, part], rs_s.at[i, j], rs_r.at[i, j],
                      (y_up if way == 0 else y_dn, e))

    def grad_start(i, left, t, own):
        owners = (lax.rem(y + 2, 4), y_up, y_dn)
        for o in range(3):
            @pl.loop(0, 2)
            def _(f):
                part, val = quarter(i, left, t, owners[o], f)
                gs[i, o, part, :] = val.astype(BF)
            if o == 0:
                rs_first(i, 0).start()
                rs_first(i, 1).start()
            elif o == 1:
                rs_second(i, 0, 1).start()
            else:
                rs_second(i, 1, 0).start()

        @pl.loop(0, 2)
        def _(f):
            part, val = quarter(i, left, t, y, f)
            own[part, :] = val

    def grad_middle(i):
        for way in range(2):
            part = pl.ds(way * fh, fh)
            rs_first(i, way).wait()
            gs[i, 1 + way, part, :] = (
                gs[i, 1 + way, part, :].astype(F32) + rs1[i, way].astype(F32)).astype(BF)
            rs_second(i, way, way).start()

    def grad_finish(i, own):
        cps = []
        for way in range(2):
            for f in range(2):
                rs_second(i, way, f).wait()
            cp = pltpu.make_async_copy(rs2.at[i, way], gs.at[i, 1 + way], in_sem.at[way])
            cp.start()
            cps.append(cp)
        for cp in cps:
            cp.wait()

        @pl.loop(0, 2)
        def _(f):
            part = pl.ds(pl.multiple_of(f * fh, fh), fh)
            own[part, :] = own[part, :] + gs[i, 1, part, :].astype(F32) + gs[i, 2, part, :].astype(F32)

    grad_start(0, h_t, 1, gd)

    @pl.loop(0, n)
    def _(b):
        cols = pl.ds(pl.multiple_of(b * blk, blk), blk)

        @pl.loop(0, 2)
        def _(f):
            part = pl.ds(pl.multiple_of(f * fh, fh), fh)
            dh = (dot_nt(w[2, part, :half], rows[1, 0, b].reshape(blk, half))
                  + dot_nt(w[2, part, half:], rows[1, 1, b].reshape(blk, half)))
            fa[part, cols] = (dh * fa[part, cols].astype(F32)).astype(BF)
            fb[part, cols] = (dh * fb[part, cols].astype(F32)).astype(BF)

    grad_middle(0)
    s2_drain(1)

    @pl.loop(0, n)
    def _(b):
        cols = pl.ds(pl.multiple_of(b * blk, blk), blk)
        dg = fa[:, cols]
        du = fb[:, cols]
        for hf in range(2):
            span = slice(hf * half, (hf + 1) * half)
            out = dot_tn(dg, w[0, :, span]) + dot_tn(du, w[1, :, span])
            snd[1, hf, b] = out.astype(BF).reshape(2, n, CAP, half)

    rt_start(1)
    grad_start(1, fa, 0, gg)

    def r1_copy(t, hf, d):
        return remote(s1.at[t, hf, d], prec.at[t, hf, d - 1], r1_s.at[t, hf, d - 1],
                      r1_r.at[t, hf, d - 1], ring_back(hf, d))

    def relay_sum(t, hf, d):
        at = down(x if hf == 0 else z, d)
        got = rel[t, hf, :, at].reshape(blk, half)
        if t == 0:
            both = dot_tn(pg[hf, d], got)
            return (both[:tokens] + both[tokens:]) * (1.0 / 65536.0)
        return dot_tn(pb[hf, d], got)

    def relay_back(t):
        @pl.loop(1, n)
        def _(d):
            for hf in range(2):
                s1[t, hf, d] = relay_sum(t, hf, d).astype(BF)
                r1_copy(t, hf, d).start()

        for hf in range(2):
            ownp[hf] = relay_sum(t, hf, 0)

    def last_sum(t, out):
        for hf in range(2):
            total = ownp[hf]
            for d in range(1, n):
                r1_copy(t, hf, d).wait()
                total = total + prec[t, hf, d - 1].astype(F32)
            out[:, hf * half:(hf + 1) * half] = total.astype(BF)

    rt_finish(0)
    relay_back(0)
    grad_start(2, fb, 0, gu)
    grad_middle(1)
    last_sum(0, mixed)
    rt_finish(1)
    relay_back(1)
    grad_middle(2)
    grad_finish(0, gd)
    last_sum(1, tgrad)
    grad_finish(1, gg)
    grad_finish(2, gu)
    rt_drain(0)
    rt_drain(1)


def shards(n, tokens, cotangent, expert_ids, gate_fixed, w_gate, w_up, w_down):
    rows, width = tokens.shape
    top = expert_ids.shape[1]
    ff = w_down.shape[1]
    half = width // 2
    quart = width // 4
    pad = ((0, 8 - top), (0, 0))
    tab = jnp.concatenate(
        [jnp.pad(expert_ids.T, pad, constant_values=-1), jnp.pad(gate_fixed.T, pad)], axis=0)
    any_spec = pl.BlockSpec(memory_space=pl.ANY)
    vm = pl.BlockSpec(memory_space=pltpu.VMEM)
    dma = pltpu.SemaphoreType.DMA
    blk = 2 * n * CAP
    slots = n * blk
    big = (2, 2, n, 2, n, CAP, half)
    grad = jax.ShapeDtypeStruct((ff, quart), F32)
    act = jax.ShapeDtypeStruct((rows, width), BF)
    outs = pl.pallas_call(
        functools.partial(layer, n, top),
        out_shape=(act, act, grad, grad, grad, jax.ShapeDtypeStruct((3, 2, ff, quart), BF)),
        in_specs=[any_spec] * 6,
        out_specs=[vm] * 5 + [any_spec],
        scratch_shapes=[
            pltpu.VMEM((3, ff, width), BF),
            pltpu.VMEM((2, 2, n, rows, half), BF),
            pltpu.VMEM((2, n, 16, rows), jnp.int32),
            pltpu.VMEM((2, n, blk, rows), BF),
            pltpu.VMEM((2, n, blk, 2 * rows), BF),
            pltpu.VMEM(big, BF),
            pltpu.VMEM(big, BF),
            pltpu.VMEM((2, 2, 2 * n, n, CAP, half), BF),
            pltpu.VMEM((2, 2, n - 1, rows, half), BF),
            pltpu.VMEM((2, rows, half), F32),
            pltpu.VMEM((ff, slots), BF),
            pltpu.VMEM((ff, slots), BF),
            pltpu.VMEM((ff, slots), BF),
            pltpu.VMEM((3, 3, ff, quart), BF),
            pltpu.VMEM((3, 2, ff // 2, quart), BF),
            dma((9,)),
            dma((2, 2, n - 1)), dma((2, 2, n - 1)),
            dma((2, n - 1)), dma((2, n - 1)),
            dma((2, 2, 2 * n - 1)), dma((2, 2, 2 * n - 1)),
            dma((2, 2, 2 * n - 1)), dma((2, 2, 2 * n - 1)),
            dma((2, 2, n - 1)), dma((2, 2, n - 1)),
            dma((3, 6)), dma((3, 6)),
            dma((4, 2)),
        ],
        compiler_params=pltpu.CompilerParams(
            collective_id=0, has_side_effects=True, vmem_limit_bytes=67043328),
    )(tab, tokens, cotangent, w_gate[0].T, w_up[0].T, w_down[0])
    mixed, tgrad, gg, gu, gd = outs[:5]
    return (mixed, tgrad, gg.T[None], gu.T[None], gd[None])


def solution(mesh):
    n = round((mesh.shape["expert"] // 2) ** 0.5)
    in_specs = (
        P(("dp", "expert"), None),
        P(("dp", "expert"), None),
        P(("dp", "expert"), None),
        P(("dp", "expert"), None),
        P("expert", None, None),
        P("expert", None, None),
        P("expert", None, None),
    )
    out_specs = (
        P(("dp", "expert"), None),
        P(("dp", "expert"), None),
        P("expert", "dp", None),
        P("expert", "dp", None),
        P("expert", None, "dp"),
    )
    return jax.shard_map(functools.partial(shards, n), mesh=mesh, in_specs=in_specs,
                         out_specs=out_specs, check_vma=False)
```

time: 353 us -> 173 us (0.49); the launches traced: 347 us -> 173 us
  Pallas kernels: 0 us -> 162 us
  waiting for transfers between devices: 147 us -> 0 us
  matrix products: 61 us -> 0 us
  local copies, waits for them, and re-layouts: 56.7 us -> 8.74 us
  other arithmetic: 36 us -> 1.31 us
  starting transfers between devices: 32.3 us -> 0 us
  between operations: 14.2 us -> 0.65 us
    pallas_call x0 -> x1, Pallas kernels: none -> 162 us  [shards(): pl.pallas_call(functools.partial(layer, n, top), out_shape=(act, act, gra...]
    all_to_all x4 -> x0, waiting for transfers between devices: 147 us -> none  [the longest x1 41.1 us: shards(): lax.all_to_all(outgoing, 'expert', split_axis=0, concat_axis=0, tiled=True)]
    dot_general x9 -> x0, matrix products: 61 us -> none  [the longest x3 20.8 us: contract(): lax.dot_general(left, right, (((0,), (0,)), ((), ())), preferred_element_...]
    gather x5 -> x0, local copies, waits for them, and re-layouts: 38.1 us -> none  [the longest x2 16.3 us: shards(): back_rows[slot_of].astype(jnp.float32).reshape(tok_rows, top_k, width)]
    all_to_all x4 -> x0, starting transfers between devices: 31.4 us -> none  [the longest x1 9.61 us: shards(): lax.all_to_all(outgoing, 'expert', split_axis=0, concat_axis=0, tiled=True)]
    reduce_sum x3 -> x0, other arithmetic: 13.3 us -> none  [the longest x1 7.54 us: shards(): jnp.sum(mixed_rows * gate_values.reshape(tok_rows, top_k)[:, :, None], ax...]
    broadcast_in_dim x3 -> x0, other arithmetic: 7.22 us -> none  [shards(): return (mixed, token_grad, grad_gate[None], grad_up[None], grad_down[None])]
    scatter x2 -> x0, local copies, waits for them, and re-layouts: 6.92 us -> none  [the longest x1 3.54 us: shards(): slot_token = jnp.zeros((slot_count,), jnp.int32).at[slot_of].set(owner)]
  transfers between devices with their start and end apart: 7 -> 0, of which waited for: 4 -> 0; matrix products, arithmetic and copies ran while one was open for 31% -> 0% of each run, Pallas kernels for 0% -> 0%
where the time goes in v1:
time: 173 us
  Pallas kernels  162 us (94%)
  local copies, waits for them, and re-layouts  8.74 us (5%)
    pallas_call x1, Pallas kernels, shards(): pl.pallas_call(functools.partial(layer, n, top), out_shape=(act, act, gra...  162 us
    unnamed x11, local copies, waits for them, and re-layouts  8.74 us

profile of v1, /device:TPU:1, one launch (start us, length us, event | category | flops | bytes accessed | tf_op | source)
XLA Modules:
  0.0 173.0 jit_solution(534951603036714214)
XLA Ops:
  0.6 1.3 pad_add_fusion.tab
  1.9 162.3 %shard_map.110 = (bf16[128,2048]{1,0:T(8,128)(2,1)}, bf16[128,2048]{1,0:T(8,128)(2,1)}, f32[704,512]{1,0:T(8,128)}, f32[704,512]{1,0:T(8,128)}, f32[704,512]{1,0:T(8,128)}, /*index=5*/bf16[3,2,704,512]{3,2,1,0:T(8,128)(2,1)}) custom-call(s32[16,128]{1,0:T(8,128)} %pad_add_fusion.tab, bf16[128,2048]{1,0:T(8,128)(2,1)} %tok.1, bf16[128,2048]{1,0:T(8,128)(2,1)} %cot.1, ...), custom_call_target="tpu_custom_call" | custom-call | tf_op jit(solution)/shard_map/pallas_call | solution.py:455
  164.2 0.0 copy-start.2
  164.2 2.0 %copy.17 = bf16[128,2048]{1,0:T(8,128)(2,1)} copy(bf16[128,2048]{1,0:T(8,128)(2,1)} %get-tuple-element.20) | data formatting | bytes 1048576
  166.2 1.9 %copy.18 = bf16[128,2048]{1,0:T(8,128)(2,1)} copy(bf16[128,2048]{1,0:T(8,128)(2,1)} %get-tuple-element.21) | data formatting | bytes 1048576
  168.1 0.0 copy-done.2
  168.1 0.0 copy-start.1
  168.1 1.1 copy.19
  169.2 0.8 copy-done.1
  170.0 0.0 copy-start
  170.0 1.1 copy.20
  171.1 0.8 copy-done
  171.9 1.1 copy.21
Async XLA Ops:
  164.2 3.9 %copy-start.2 = (f32[704,512]{1,0:T(8,128)S(1)}, f32[704,512]{1,0:T(8,128)}, u32[]{:S(2)}) copy-start(f32[704,512]{1,0:T(8,128)} %get-tuple-element.12) | copy-start | bytes 4325380
  168.1 1.9 %copy-start.1 = (f32[704,512]{1,0:T(8,128)S(1)}, f32[704,512]{1,0:T(8,128)}, u32[]{:S(2)}) copy-start(f32[704,512]{1,0:T(8,128)} %get-tuple-element.13) | copy-start | bytes 4325380
  170.0 1.9 %copy-start = (f32[704,512]{1,0:T(8,128)S(1)}, f32[704,512]{1,0:T(8,128)}, u32[]{:S(2)}) copy-start(f32[704,512]{1,0:T(8,128)} %get-tuple-element.14) | copy-start | bytes 4325380

commit v2 on v1

v2 whole, which is shorter than its diff:
```python
import functools

import jax
import jax.numpy as jnp
from jax import lax
from jax.experimental import pallas as pl
from jax.experimental.pallas import tpu as pltpu
from jax.sharding import PartitionSpec as P

MESH = pl.DeviceIdType.MESH
CAP = 32
N = 4
BF = jnp.bfloat16
F32 = jnp.float32


def dot_nn(a, b):
    return lax.dot_general(a, b, (((1,), (0,)), ((), ())), preferred_element_type=F32)


def dot_nt(a, b):
    return lax.dot_general(a, b, (((1,), (1,)), ((), ())), preferred_element_type=F32)


def dot_tn(a, b):
    return lax.dot_general(a, b, (((0,), (0,)), ((), ())), preferred_element_type=F32)


def layer(top, tab, tok, cot, wg, wu, wd, mixed, tgrad, own_out, rs2,
          w, s1, tb, pb, pg, snd, rows, rel, p1, p2, ownp, h_t, fa, fb, gs, rs1, own, mix, tgr,
          in_sem, s1_s, s1_r, tb_s, tb_r, s2_s, s2_r, rt_s, rt_r, r1_s, r1_r,
          rs_s, rs_r, loc, out_sem):
    n = N
    tokens, width = tok.shape
    half = width // 2
    th = tokens // 2
    ff = w.shape[2]
    fh = ff // 2
    quart = width // 4
    piece = width // 8
    blk = 2 * n * CAP
    slots = n * blk
    y = lax.axis_index("dp")
    e = lax.axis_index("expert")
    x = e // (2 * n)
    z = lax.rem(e // 2, n)
    c = lax.rem(e, 2)

    def dev(xx, zz, cc):
        return (y, xx * (2 * n) + zz * 2 + cc)

    def up(v, d):
        return lax.rem(v + d, n)

    def down(v, d):
        return lax.rem(v + n - d, n)

    def ring(hf, d):
        return dev(up(x, d), z, c) if hf == 0 else dev(x, up(z, d), c)

    y_up = lax.rem(y + 1, 4)
    y_dn = lax.rem(y + 3, 4)
    offsets = [(d, k) for d in range(n) for k in range(2) if (d, k) != (0, 0)]

    pltpu.make_async_copy(tab, tb.at[0, 0], in_sem.at[0]).start()
    pltpu.make_async_copy(tab, tb.at[1, 0], in_sem.at[1]).start()

    def columns(hf):
        for ab in range(2):
            for j in range(2):
                yield (pl.ds((2 * hf + j) * quart + ab * piece, piece),
                       pl.ds((2 * ab + j) * piece, piece))

    for t, src in enumerate((tok, cot)):
        for hf in range(2):
            for there, here in columns(hf):
                pltpu.make_async_copy(src.at[:, there], s1.at[t, hf, 0, :, here],
                                      in_sem.at[2 + 2 * t + hf]).start()
    for i, src in enumerate((wg, wu, wd)):
        for hf in range(2):
            for there, here in columns(hf):
                pltpu.make_async_copy(src.at[:, there], w.at[i, hf, :, here],
                                      in_sem.at[6 + 2 * i + hf]).start()

    def in_wait(t, hf):
        pltpu.make_async_copy(tok.at[:, pl.ds(0, half)], s1.at[t, hf, 0], in_sem.at[2 + 2 * t + hf]).wait()

    bar = pltpu.get_barrier_semaphore()
    partners = []
    for d, k in offsets:
        partners.append(dev(x, up(z, d), lax.rem(c + k, 2)))
        if d > 0:
            partners.append(dev(up(x, d), z, lax.rem(c + k, 2)))
    partners.append((y_up, e))
    partners.append((y_dn, e))
    for p in partners:
        pl.semaphore_signal(bar, inc=1, device_id=p, device_id_type=MESH)
    pl.semaphore_wait(bar, len(partners))

    def remote(src, dst, s, r, d):
        return pltpu.make_async_remote_copy(
            src_ref=src, dst_ref=dst, send_sem=s, recv_sem=r, device_id=d, device_id_type=MESH)

    def tab_copy(hf, d):
        return remote(tb.at[hf, 0], tb.at[hf, d], tb_s.at[hf, d - 1], tb_r.at[hf, d - 1], ring(hf, d))

    def s1_copy(t, hf, way):
        d = 1 if way == 0 else 3
        return remote(s1.at[t, hf, 0], s1.at[t, hf, d], s1_s.at[t, hf, way],
                      s1_r.at[t, hf, way], ring(hf, d))

    def s1_pass(t, hf, way):
        d = 1 if way == 0 else 3
        part = pl.ds(way * th, th)
        return remote(s1.at[t, hf, d, part], s1.at[t, hf, 2, part], s1_s.at[t, hf, 2 + way],
                      s1_r.at[t, hf, 2 + way], ring(hf, d))

    pltpu.make_async_copy(tab, tb.at[0, 0], in_sem.at[0]).wait()
    pltpu.make_async_copy(tab, tb.at[1, 0], in_sem.at[1]).wait()
    for hf in range(2):
        for d in range(1, n):
            tab_copy(hf, d).start()
    for t in range(2):
        for hf in range(2):
            in_wait(t, hf)
            for way in range(2):
                s1_copy(t, hf, way).start()

    upper = (lax.broadcasted_iota(jnp.int32, (tokens, tokens), 0)
             < lax.broadcasted_iota(jnp.int32, (tokens, tokens), 1))
    upper = jnp.where(upper, 1.0, 0.0).astype(BF)
    row16 = lax.broadcasted_iota(jnp.int32, (16, tokens), 0)
    slot_no = lax.broadcasted_iota(jnp.int32, (CAP, tokens), 0).astype(F32)

    def make_p(hf, d):
        if hf == 0:
            names = x * (2 * n) + row16
        else:
            names = lax.shift_right_logical(row16, 1) * (2 * n) + z * 2 + lax.bitwise_and(row16, 1)
        table = tb[hf, d]
        hit = jnp.zeros((16, tokens), F32)
        gate = jnp.zeros((16, tokens), jnp.int32)
        for k in range(top):
            same = table[k:k + 1, :] == names
            hit = jnp.where(same, 1.0, hit)
            gate = jnp.where(same, table[8 + k:9 + k, :], gate)
        rank = dot_nn(hit.astype(BF), upper)
        rank = jnp.where(hit > 0.0, rank, -1.0)
        high = (lax.shift_right_logical(gate, 8) * 256).astype(F32)
        low = lax.bitwise_and(gate, 255).astype(F32)
        for i in range(2 * n):
            one = slot_no == rank[i:i + 1, :]
            at = pl.ds(i * CAP, CAP)
            pb[hf, d, at, :] = jnp.where(one, 1.0, 0.0).astype(BF)
            pg[hf, d, at, pl.ds(0, tokens)] = jnp.where(one, high[i:i + 1, :], 0.0).astype(BF)
            pg[hf, d, at, pl.ds(tokens, tokens)] = jnp.where(one, low[i:i + 1, :], 0.0).astype(BF)

    def relay_out(t, hf, d):
        at = down(x if hf == 0 else z, d)
        src = s1[t, hf, d]
        if t == 0:
            picked = dot_nn(pb[hf, d], src)
        else:
            picked = dot_nn(pg[hf, d], jnp.concatenate([src, src], axis=0)) * (1.0 / 65536.0)
        snd[t, hf, :, :, at] = picked.astype(BF).reshape(n, 2, CAP, half)

    for hf in range(2):
        make_p(hf, 0)
        relay_out(0, hf, 0)

    @pl.loop(1, n)
    def _(d):
        for hf in range(2):
            tab_copy(hf, d).wait()
            make_p(hf, d)

    for hf in range(2):
        for way in range(2):
            s1_copy(0, hf, way).wait()
            s1_pass(0, hf, way).start()
    for hf in range(2):
        relay_out(0, hf, 1)
        relay_out(0, hf, 3)
    for hf in range(2):
        for way in range(2):
            s1_copy(1, hf, way).wait()
            s1_pass(1, hf, way).start()

    def s2_copy(u, hf, d, k):
        j = 2 * d + k - 1
        cd = lax.rem(c + k, 2)
        t = min(u, 1)
        cols = pl.ds(0, half) if u == 0 else pl.ds((u - 1) * quart, quart)
        if hf == 0:
            zd = up(z, d)
            return remote(snd.at[t, 0, zd, cd, :, :, cols], rows.at[t, 0, z, c, :, :, cols],
                          s2_s.at[u, 0, j], s2_r.at[u, 0, j], dev(x, zd, cd))
        xd = up(x, d)
        return remote(snd.at[t, 1, xd, cd, :, :, cols], rows.at[t, 1, :, c, x, :, cols],
                      s2_s.at[u, 1, j], s2_r.at[u, 1, j], dev(xd, z, cd))

    def s2_wait(u, hf, d, k):
        j = 2 * d + k - 1
        cf = lax.rem(c + k, 2)
        t = min(u, 1)
        cols = pl.ds(0, half) if u == 0 else pl.ds((u - 1) * quart, quart)
        if hf == 0:
            land = rows.at[t, 0, down(z, d), cf, :, :, cols]
        else:
            land = rows.at[t, 1, :, cf, down(x, d), :, cols]
        remote(land, land, s2_s.at[u, hf, j], s2_r.at[u, hf, j], dev(x, up(z, 1), c)).wait_recv()

    def s2_self(t, hf):
        if hf == 0:
            return pltpu.make_async_copy(snd.at[t, 0, z, c], rows.at[t, 0, z, c], loc.at[t, 0])
        return pltpu.make_async_copy(snd.at[t, 1, x, c], rows.at[t, 1, :, c, x], loc.at[t, 1])

    def s2_start(u):
        for d, k in offsets:
            for hf in range(2):
                s2_copy(u, hf, d, k).start()

    def s2_finish(u):
        for d, k in offsets:
            for hf in range(2):
                s2_wait(u, hf, d, k)

    def s2_drain(u):
        for d, k in offsets:
            for hf in range(2):
                s2_copy(u, hf, d, k).wait_send()

    for hf in range(2):
        for way in range(2):
            s1_pass(0, hf, way).wait()
        relay_out(0, hf, 2)
    s2_start(0)
    for hf in range(2):
        s2_self(0, hf).start()
    for hf in range(2):
        relay_out(1, hf, 0)
        relay_out(1, hf, 1)
        relay_out(1, hf, 3)
    for hf in range(2):
        for way in range(2):
            s1_pass(1, hf, way).wait()
        relay_out(1, hf, 2)
    s2_start(1)
    s2_start(2)
    for hf in range(2):
        s2_self(1, hf).start()

    for i, src in enumerate((wg, wu, wd)):
        for hf in range(2):
            pltpu.make_async_copy(src.at[:, pl.ds(0, half)], w.at[i, hf], in_sem.at[6 + 2 * i + hf]).wait()
    s2_finish(0)
    for hf in range(2):
        s2_self(0, hf).wait()

    @pl.loop(0, n)
    def _(b):
        cols = pl.ds(pl.multiple_of(b * blk, blk), blk)

        @pl.loop(0, 2)
        def _(f):
            part = pl.ds(pl.multiple_of(f * fh, fh), fh)
            xa = rows[0, 0, b].reshape(blk, half)
            xb = rows[0, 1, b].reshape(blk, half)
            gate = dot_nt(w[0, 0, part, :], xa) + dot_nt(w[0, 1, part, :], xb)
            upv = dot_nt(w[1, 0, part, :], xa) + dot_nt(w[1, 1, part, :], xb)
            s = jax.nn.sigmoid(gate)
            act = gate * s
            h_t[part, cols] = (act * upv).astype(BF)
            fa[part, cols] = (upv * (s * (1.0 + gate * (1.0 - s)))).astype(BF)
            fb[part, cols] = act.astype(BF)

    def quarter(left, t, ab, q, f):
        part = pl.ds(pl.multiple_of(f * fh, fh), fh)
        cols = pl.ds(pl.multiple_of(ab * quart + lax.rem(q, 2) * piece, piece), piece)
        right = rows[t, q // 2, :, :, :, :, cols].reshape(slots, piece)
        return part, dot_nn(left[part, :], right)

    def rs_first(i, ab, way):
        part = pl.ds(way * fh, fh)
        return remote(gs.at[i, ab, 0, part], rs1.at[i, ab, way], rs_s.at[i, ab, way],
                      rs_r.at[i, ab, way], (y_up if way == 0 else y_dn, e))

    def rs_second(i, ab, way, f):
        part = pl.ds(f * fh, fh)
        j = 2 + 2 * way + f
        return remote(gs.at[i, ab, 1 + way, part], rs2.at[i, ab, way, part], rs_s.at[i, ab, j],
                      rs_r.at[i, ab, j], (y_up if way == 0 else y_dn, e))

    def grad_send(i, ab, left, t):
        owners = (lax.rem(y + 2, 4), y_up, y_dn)
        for o in range(3):
            @pl.loop(0, 2)
            def _(f):
                part, val = quarter(left, t, ab, owners[o], f)
                gs[i, ab, o, part, :] = val.astype(BF)
            if o == 0:
                rs_first(i, ab, 0).start()
                rs_first(i, ab, 1).start()
            elif o == 1:
                rs_second(i, ab, 0, 1).start()
            else:
                rs_second(i, ab, 1, 0).start()

    def grad_own(i, ab, left, t):
        @pl.loop(0, 2)
        def _(f):
            part, val = quarter(left, t, ab, y, f)
            own[i, part, pl.ds(ab * piece, piece)] = val

    def grad_middle(i, ab):
        for way in range(2):
            part = pl.ds(way * fh, fh)
            rs_first(i, ab, way).wait()
            gs[i, ab, 1 + way, part, :] = (
                gs[i, ab, 1 + way, part, :].astype(F32) + rs1[i, ab, way].astype(F32)).astype(BF)
            rs_second(i, ab, way, way).start()

    def rs_wait(i, ab):
        for way in range(2):
            for f in range(2):
                rs_second(i, ab, way, f).wait()

    def grad_finish(i):
        def stage(ab, way):
            return pltpu.make_async_copy(rs2.at[i, ab, way], gs.at[i, ab, 1 + way], out_sem.at[2 * ab + way])

        for ab in range(2):
            rs_wait(i, ab)
            for way in range(2):
                stage(ab, way).start()
        for ab in range(2):
            for way in range(2):
                stage(ab, way).wait()

            @pl.loop(0, 2)
            def _(f):
                part = pl.ds(pl.multiple_of(f * fh, fh), fh)
                cols = pl.ds(ab * piece, piece)
                own[i, part, cols] = (own[i, part, cols] + gs[i, ab, 1, part, :].astype(F32)
                                      + gs[i, ab, 2, part, :].astype(F32))

    def own_copy(i):
        return pltpu.make_async_copy(own.at[i], own_out.at[i], out_sem.at[4 + i])

    s2_finish(1)
    for hf in range(2):
        s2_self(1, hf).wait()
    grad_send(0, 0, h_t, 1)
    s2_drain(0)

    @pl.loop(0, n)
    def _(b):
        hid = h_t[:, pl.ds(pl.multiple_of(b * blk, blk), blk)]
        for hf in range(2):
            snd[0, hf, b] = dot_tn(hid, w[2, hf]).astype(BF).reshape(2, n, CAP, half)

    def rt_copy(t, hf, d, k):
        j = 2 * d + k - 1
        cd = lax.rem(c + k, 2)
        if hf == 0:
            zd = up(z, d)
            return remote(snd.at[t, 0, zd, cd], rel.at[t, 0, z * 2 + c], rt_s.at[t, 0, j],
                          rt_r.at[t, 0, j], dev(x, zd, cd))
        xd = up(x, d)
        return remote(snd.at[t, 1, :, cd, xd], rel.at[t, 1, x * 2 + c], rt_s.at[t, 1, j],
                      rt_r.at[t, 1, j], dev(xd, z, cd))

    def rt_wait(t, hf, d, k):
        j = 2 * d + k - 1
        cf = lax.rem(c + k, 2)
        land = rel.at[t, hf, down(z if hf == 0 else x, d) * 2 + cf]
        remote(land, land, rt_s.at[t, hf, j], rt_r.at[t, hf, j], dev(x, up(z, 1), c)).wait_recv()

    def rt_self(t, hf):
        if hf == 0:
            return pltpu.make_async_copy(snd.at[t, 0, z, c], rel.at[t, 0, z * 2 + c], loc.at[2 + t, 0])
        return pltpu.make_async_copy(snd.at[t, 1, :, c, x], rel.at[t, 1, x * 2 + c], loc.at[2 + t, 1])

    def rt_start(t):
        for d, k in offsets:
            for hf in range(2):
                rt_copy(t, hf, d, k).start()
        for hf in range(2):
            rt_self(t, hf).start()

    def rt_finish(t):
        for d, k in offsets:
            for hf in range(2):
                rt_wait(t, hf, d, k)
        for hf in range(2):
            rt_self(t, hf).wait()

    def rt_drain(t):
        for d, k in offsets:
            for hf in range(2):
                rt_copy(t, hf, d, k).wait_send()

    rt_start(0)
    grad_middle(0, 0)
    s2_finish(2)
    grad_send(0, 1, h_t, 1)

    @pl.loop(0, n)
    def _(b):
        cols = pl.ds(pl.multiple_of(b * blk, blk), blk)

        @pl.loop(0, 2)
        def _(f):
            part = pl.ds(pl.multiple_of(f * fh, fh), fh)
            dh = (dot_nt(w[2, 0, part, :], rows[1, 0, b].reshape(blk, half))
                  + dot_nt(w[2, 1, part, :], rows[1, 1, b].reshape(blk, half)))
            fa[part, cols] = (dh * fa[part, cols].astype(F32)).astype(BF)
            fb[part, cols] = (dh * fb[part, cols].astype(F32)).astype(BF)

    grad_middle(0, 1)
    grad_send(1, 0, fa, 0)
    s2_drain(1)
    s2_drain(2)

    @pl.loop(0, n)
    def _(b):
        cols = pl.ds(pl.multiple_of(b * blk, blk), blk)
        dg = fa[:, cols]
        du = fb[:, cols]
        for hf in range(2):
            out = dot_tn(dg, w[0, hf]) + dot_tn(du, w[1, hf])
            snd[1, hf, b] = out.astype(BF).reshape(2, n, CAP, half)

    rt_start(1)
    grad_middle(1, 0)
    grad_send(1, 1, fa, 0)

    def r1_first(t, hf, way):
        part = pl.ds(way * th, th)
        return remote(s1.at[t, hf, 2, part], p1.at[t, hf, way], r1_s.at[t, hf, way],
                      r1_r.at[t, hf, way], ring(hf, 3 if way == 0 else 1))

    def r1_second(t, hf, way, f):
        part = pl.ds(f * th, th)
        j = 2 + 2 * way + f
        return remote(s1.at[t, hf, 1 if way == 0 else 3, part], p2.at[t, hf, way, part],
                      r1_s.at[t, hf, j], r1_r.at[t, hf, j], ring(hf, 3 if way == 0 else 1))

    def relay_sum(t, hf, d):
        at = down(x if hf == 0 else z, d)
        got = rel[t, hf, :, at].reshape(blk, half)
        if t == 0:
            both = dot_tn(pg[hf, d], got)
            return (both[:tokens] + both[tokens:]) * (1.0 / 65536.0)
        return dot_tn(pb[hf, d], got)

    def relay_back(t):
        for hf in range(2):
            s1[t, hf, 2] = relay_sum(t, hf, 2).astype(BF)
            for way in range(2):
                r1_first(t, hf, way).start()
        for hf in range(2):
            for way in range(2):
                d = 1 if way == 0 else 3
                s1[t, hf, d] = relay_sum(t, hf, d).astype(BF)
                r1_second(t, hf, way, 1 - way).start()

    def relay_own(t):
        for hf in range(2):
            ownp[hf] = relay_sum(t, hf, 0)

    def relay_middle(t):
        for hf in range(2):
            for way in range(2):
                d = 1 if way == 0 else 3
                part = pl.ds(way * th, th)
                r1_first(t, hf, way).wait()
                s1[t, hf, d, part, :] = (
                    s1[t, hf, d, part, :].astype(F32) + p1[t, hf, way].astype(F32)).astype(BF)
                r1_second(t, hf, way, way).start()

    def last_sum(t, out):
        for hf in range(2):
            for way in range(2):
                for f in range(2):
                    r1_second(t, hf, way, f).wait()
            total = (ownp[hf] + p2[t, hf, 0].astype(F32) + p2[t, hf, 1].astype(F32)).astype(BF)
            for ab in range(2):
                for j in range(2):
                    at = (2 * hf + j) * quart + ab * piece
                    src = (2 * ab + j) * piece
                    out[:, at:at + piece] = total[:, src:src + piece]

    grad_own(0, 0, h_t, 1)
    grad_own(0, 1, h_t, 1)
    rt_finish(0)
    relay_back(0)
    grad_middle(1, 1)
    grad_send(2, 0, fb, 0)
    relay_middle(0)
    relay_own(0)
    grad_middle(2, 0)
    grad_send(2, 1, fb, 0)
    for ab in range(2):
        grad_own(1, ab, fa, 0)
        grad_own(2, ab, fb, 0)
    own_copy(2).start()
    last_sum(0, mix)
    mixed_out = pltpu.make_async_copy(mix, mixed, out_sem.at[7])
    mixed_out.start()
    grad_middle(2, 1)
    grad_finish(0)
    own_copy(0).start()
    rt_finish(1)
    relay_back(1)
    relay_own(1)
    relay_middle(1)
    grad_finish(1)
    own_copy(1).start()
    last_sum(1, tgr)
    tgrad_out = pltpu.make_async_copy(tgr, tgrad, out_sem.at[8])
    tgrad_out.start()
    rt_drain(0)
    rt_drain(1)
    rs_wait(2, 0)
    rs_wait(2, 1)
    for i in range(3):
        own_copy(i).wait()
    mixed_out.wait()
    tgrad_out.wait()


def finish(mixed, tgrad, own, rs2, mixed_out, tgrad_out, gg, gu, gd):
    mixed_out[...] = mixed[...]
    tgrad_out[...] = tgrad[...]
    gd[...] = own[0]
    gg[...] = own[1]
    piece = rs2.shape[-1]
    for ab in range(2):
        cols = slice(ab * piece, (ab + 1) * piece)
        gu[:, cols] = own[2, :, cols] + rs2[0, ab, 0].astype(F32) + rs2[0, ab, 1].astype(F32)


def shards(tokens, cotangent, expert_ids, gate_fixed, w_gate, w_up, w_down):
    rows, width = tokens.shape
    top = expert_ids.shape[1]
    ff = w_down.shape[1]
    half = width // 2
    quart = width // 4
    pad = ((0, 8 - top), (0, 0))
    tab = jnp.concatenate(
        [jnp.pad(expert_ids.T, pad, constant_values=-1), jnp.pad(gate_fixed.T, pad)], axis=0)
    any_spec = pl.BlockSpec(memory_space=pl.ANY)
    dma = pltpu.SemaphoreType.DMA
    n = N
    blk = 2 * n * CAP
    slots = n * blk
    piece = width // 8
    big = (2, 2, n, 2, n, CAP, half)
    grad = jax.ShapeDtypeStruct((ff, quart), F32)
    act = jax.ShapeDtypeStruct((rows, width), BF)
    parts = pl.pallas_call(
        functools.partial(layer, top),
        out_shape=(act, act, jax.ShapeDtypeStruct((3, ff, quart), F32),
                   jax.ShapeDtypeStruct((3, 2, 2, ff, piece), BF)),
        in_specs=[any_spec] * 6,
        out_specs=[any_spec] * 4,
        scratch_shapes=[
            pltpu.VMEM((3, 2, ff, half), BF),
            pltpu.VMEM((2, 2, n, rows, half), BF),
            pltpu.VMEM((2, n, 16, rows), jnp.int32),
            pltpu.VMEM((2, n, blk, rows), BF),
            pltpu.VMEM((2, n, blk, 2 * rows), BF),
            pltpu.VMEM(big, BF),
            pltpu.VMEM(big, BF),
            pltpu.VMEM((2, 2, 2 * n, n, CAP, half), BF),
            pltpu.VMEM((2, 2, 2, rows // 2, half), BF),
            pltpu.VMEM((2, 2, 2, rows, half), BF),
            pltpu.VMEM((2, rows, half), F32),
            pltpu.VMEM((ff, slots), BF),
            pltpu.VMEM((ff, slots), BF),
            pltpu.VMEM((ff, slots), BF),
            pltpu.VMEM((3, 2, 3, ff, piece), BF),
            pltpu.VMEM((3, 2, 2, ff // 2, piece), BF),
            pltpu.VMEM((3, ff, quart), F32),
            pltpu.VMEM((rows, width), BF),
            pltpu.VMEM((rows, width), BF),
            dma((12,)),
            dma((2, 2, 4)), dma((2, 2, 4)),
            dma((2, n - 1)), dma((2, n - 1)),
            dma((3, 2, 2 * n - 1)), dma((3, 2, 2 * n - 1)),
            dma((2, 2, 2 * n - 1)), dma((2, 2, 2 * n - 1)),
            dma((2, 2, 6)), dma((2, 2, 6)),
            dma((3, 2, 6)), dma((3, 2, 6)),
            dma((4, 2)),
            dma((9,)),
        ],
        compiler_params=pltpu.CompilerParams(
            collective_id=0, has_side_effects=True, vmem_limit_bytes=67043328),
    )(tab, tokens, cotangent, w_gate[0].T, w_up[0].T, w_down[0])
    steps = 4
    fs = ff // steps
    act_spec = pl.BlockSpec((rows // steps, width), lambda i: (i, 0))
    grad_spec = pl.BlockSpec((fs, quart), lambda i: (i, 0))
    mixed, tgrad, gg, gu, gd = pl.pallas_call(
        finish,
        grid=(steps,),
        out_shape=(act, act, grad, grad, grad),
        in_specs=[act_spec, act_spec, pl.BlockSpec((3, fs, quart), lambda i: (0, i, 0)),
                  pl.BlockSpec((1, 2, 2, fs, piece), lambda i: (2, 0, 0, i, 0))],
        out_specs=[act_spec, act_spec, grad_spec, grad_spec, grad_spec],
    )(*parts)
    return (mixed, tgrad, gg.T[None], gu.T[None], gd[None])


def solution(mesh):
    in_specs = (
        P(("dp", "expert"), None),
        P(("dp", "expert"), None),
        P(("dp", "expert"), None),
        P(("dp", "expert"), None),
        P("expert", None, None),
        P("expert", None, None),
        P("expert", None, None),
    )
    out_specs = (
        P(("dp", "expert"), None),
        P(("dp", "expert"), None),
        P("expert", "dp", None),
        P("expert", "dp", None),
        P("expert", None, "dp"),
    )
    return jax.shard_map(shards, mesh=mesh, in_specs=in_specs,
                         out_specs=out_specs, check_vma=False)
```

time: 173 us -> 157 us (0.908)
  local copies, waits for them, and re-layouts: 8.74 us -> 0 us
  Pallas kernels: 162 us -> 155 us
    unnamed x11 -> x0, local copies, waits for them, and re-layouts: 8.74 us -> none
    pallas_call x1 -> x2, Pallas kernels: 162 us -> 155 us  [the longest x1 150 us: shards(): pl.pallas_call(functools.partial(layer, top), out_shape=(act, act, jax.Sh...]
where the time goes in v2:
time: 157 us
  Pallas kernels  155 us (99%)
    pallas_call x1, Pallas kernels, shards(): pl.pallas_call(functools.partial(layer, top), out_shape=(act, act, jax.Sh...  150 us
    pallas_call x1, Pallas kernels, shards(): pl.pallas_call(finish, grid=(steps,), out_shape=(act, act, grad, grad, gr...  5.66 us

profile of v2, /device:TPU:1, one launch (start us, length us, event | category | flops | bytes accessed | tf_op | source)
XLA Modules:
  0.0 157.3 jit_solution(16674490998847557583)
XLA Ops:
  0.6 1.3 pad_add_fusion.tab
  1.9 149.7 %shard_map.110 = (bf16[128,2048]{1,0:T(8,128)(2,1)}, bf16[128,2048]{1,0:T(8,128)(2,1)}, f32[3,704,512]{2,1,0:T(8,128)}, bf16[3,2,2,704,256]{4,3,2,1,0:T(8,128)(2,1)}) custom-call(s32[16,128]{1,0:T(8,128)} %pad_add_fusion.tab, bf16[128,2048]{1,0:T(8,128)(2,1)} %tok.1, bf16[128,2048]{1,0:T(8,128)(2,1)} %cot.1, bf16[704,2048]{1,0:T(8,128)(2,1)} %bitcast.16, ...), custom_call_target="tpu_custom_call" | custom-call | tf_op jit(solution)/shard_map/pallas_call | solution.py:562
  151.6 5.7 %shard_map.111 = (bf16[128,2048]{1,0:T(8,128)(2,1)}, bf16[128,2048]{1,0:T(8,128)(2,1)}, f32[704,512]{1,0:T(8,128)}, f32[704,512]{1,0:T(8,128)}, f32[704,512]{1,0:T(8,128)}) custom-call(bf16[128,2048]{1,0:T(8,128)(2,1)} %get-tuple-element.14.mixed, bf16[128,2048]{1,0:T(8,128)(2,1)} %get-tuple-element.15.tgrad, f32[3,704,512]{2,1,0:T(8,128)} %get-tuple-element.16.own, ...), custom_call_target="tpu_custom_call" | custom-call | tf_op jit(solution)/shard_map/pallas_call | solution.py:605
